TPU v7x, 32 devices: a whole 2x2x4 slice. The times are simulated.
32 devices in a mesh: dp: 8 (over y, x, core), mp: 4 (over z).
Axes of the slice: x: 2, y: 2, z: 4, core: 2. Of those that a mesh axis runs over, the one named last changes fastest.
Arguments:
- features: bfloat16 [4, 4096, 1152], P('mp', 'dp'), may hold values from -6 to 6
- context_gain: float32 [1152], replicated, may hold values from 0.1 to 1.9
- queries: bfloat16 [64, 1536], replicated, may hold values from -136 to 136
- w_key: bfloat16 [1152, 384], replicated, may hold values from -0.1875 to 0.1875
- w_value: bfloat16 [1152, 384], replicated, may hold values from -0.1875 to 0.1875
- w_out: bfloat16 [1536, 2048], replicated, may hold values from -0.15625 to 0.15625
- image_tiles: int32 [4, 2], P('mp'), may hold values from 1024 to 3072, as said below
- slot_start: int32 [4, 2], P('mp'), may hold values from 0 to 64
- text_rows: bfloat16 [4, 1024, 2048], P('mp', 'dp'), may hold values from -6 to 6
- row_grads: bfloat16 [4, 1024, 2048], P('mp', 'dp'), may hold values from -6 to 6
Outputs:
- merged_rows: bfloat16 [4, 1024, 2048], P('mp', 'dp')
- query_grad: float32 [64, 1536], replicated
Inputs may be any that keep to these rules, and one draw needn't show every extreme that they name: `image_tiles`: the 2 images of a group fill its 4096 rows in order; every image takes 2 * 512 to 3072 rows, and in every group one image takes exactly 1024 and one exactly 3072.
All inputs are finite; a program needn't handle non-finite values.
Results may differ from a plain program's by a relative error of at most 0.005.
The roundings to bfloat16 on the way count: a program that leaves them out, or rounds other values in their place, can miss the bound.
Values may be sent and summed in bfloat16 or wider, within the bound.
A program may use at most 128 MiB of HBM per device.

v0:
```python
import functools

import jax
import jax.numpy as jnp
from jax import lax
from jax.experimental import pallas as pl
from jax.experimental.pallas import tpu as pltpu
from jax.sharding import PartitionSpec as P

HEADS = 16
HEAD = 96
KVH = 4
PER = HEADS // KVH
epsilon = 1e-06
LOW = -1e30
MESH = pl.DeviceIdType.MESH
F32 = jnp.float32
BF16 = jnp.bfloat16


def to_cols(rows):
    stacked = jnp.concatenate([rows[:, c * HEAD : (c + 1) * HEAD] for c in range(PER)], axis=0)
    return stacked.T


def to_rows(cols, lat):
    flipped = cols.T
    return jnp.concatenate(
        [
            flipped[c * lat : (c + 1) * lat, g * HEAD : (g + 1) * HEAD]
            for g in range(KVH)
            for c in range(PER)
        ],
        axis=1,
    )


def dot(a, b):
    return jnp.dot(a, b, preferred_element_type=F32)


class Gather:
    def __init__(self, chips, chip, core, at, send, recv):
        self.chips, self.chip, self.core = chips, chip, core
        self.at, self.send, self.recv = at, send, recv

    def hop(self, slot_chip, sem, target):
        ref = self.at(slot_chip, self.core)
        return pltpu.make_async_remote_copy(
            src_ref=ref,
            dst_ref=ref,
            send_sem=self.send.at[sem],
            recv_sem=self.recv.at[sem],
            device_id={"dp": target},
            device_id_type=MESH,
        )

    def start(self):
        for k in range(1, self.chips):
            there = lax.rem(self.chip + k, self.chips)
            self.hop(self.chip, k, there * 2 + self.core).start()
        self.hop(self.chip, 0, self.chip * 2 + 1 - self.core).start()

    def forward(self):
        for k in range(1, self.chips):
            origin = lax.rem(self.chip + self.chips - k, self.chips)
            self.hop(origin, k, origin * 2 + self.core).wait_recv()
            self.hop(origin, self.chips - 1 + k, self.chip * 2 + 1 - self.core).start()

    def finish(self):
        mate = self.chip * 2 + 1 - self.core
        for k in range(self.chips):
            origin = lax.rem(self.chip + self.chips - k, self.chips)
            ref = self.at(origin, 1 - self.core)
            sem = 0 if k == 0 else self.chips - 1 + k
            pltpu.make_async_remote_copy(
                src_ref=ref,
                dst_ref=ref,
                send_sem=self.send.at[sem],
                recv_sem=self.recv.at[sem],
                device_id={"dp": mate},
                device_id_type=MESH,
            ).wait_recv()
        for sem in range(2 * self.chips - 1):
            self.hop(self.chip, sem, mate).wait_send()


class Direct:
    def __init__(self, chips, chip, core, src, dst, send, recv):
        self.chips, self.chip, self.core = chips, chip, core
        self.src, self.dst, self.send, self.recv = src, dst, send, recv

    def hop(self, k, q, origin, target):
        return pltpu.make_async_remote_copy(
            src_ref=self.src(*target),
            dst_ref=self.dst(*origin),
            send_sem=self.send.at[2 * k + q],
            recv_sem=self.recv.at[2 * k + q],
            device_id={"dp": target[0] * 2 + target[1]},
            device_id_type=MESH,
        )

    def other(self, k, q):
        return (lax.rem(self.chip + k, self.chips), 1 - self.core if q else self.core)

    def start(self, k, q):
        self.hop(k, q, (self.chip, self.core), self.other(k, q)).start()

    def all_start(self):
        for k in list(range(1, self.chips)) + [0]:
            for q in range(2):
                if k or q:
                    self.start(k, q)

    def finish(self):
        for k in range(self.chips):
            for q in range(2):
                if k or q:
                    origin = self.other(self.chips - k, q)
                    self.hop(k, q, origin, origin).wait_recv()
        for k in range(self.chips):
            for q in range(2):
                if k or q:
                    self.hop(k, q, (self.chip, self.core), self.other(k, q)).wait_send()


def kernel(
    dims,
    tiles,
    slots,
    gain,
    queries,
    features_hbm,
    wk_hbm,
    wv_hbm,
    wo_hbm,
    text_hbm,
    grads_hbm,
    merged,
    query_grad,
    features,
    wk,
    wv,
    wo,
    text,
    grads,
    keys,
    values,
    keys_t,
    values_t,
    query_t,
    weights,
    chosen,
    sums,
    u_own,
    u_recv,
    u_all,
    stats,
    dots,
    rescale,
    g_own,
    g_chip,
    z_all,
    g_all,
    a_own,
    a_recv,
    a_pair,
    a_chip,
    a_all,
    load_sem,
    pair_send,
    pair_recv,
    u_send,
    u_got,
    s_send,
    s_got,
    d_send,
    d_got,
    gc_send,
    gc_got,
    z_send,
    z_got,
    g_send,
    g_got,
    ac_send,
    ac_got,
    a_send,
    a_got,
):
    n_dp, n_mp, images, lat, tok, seq = dims
    chips = n_dp // 2
    me = lax.axis_index("dp")
    z = lax.axis_index("mp")
    chip = lax.div(me, 2)
    core = lax.rem(me, 2)
    mate = chip * 2 + 1 - core
    scale = HEAD ** (-0.5)
    half = KVH * HEAD // 2
    block = KVH * HEAD

    loads = []

    def load(src, dst, at):
        copy = pltpu.make_async_copy(src, dst, load_sem.at[at])
        copy.start()
        return copy

    def load_out(at, g):
        part = pl.ds(pl.multiple_of(g * block, block), block)
        return load(wo_hbm.at[part], wo.at[part], 2 + at)

    half_groups = KVH // 2
    order = [(1 - core) * half_groups + t for t in range(half_groups)]
    order += [core * half_groups + t for t in range(half_groups)]
    grads_in = load(grads_hbm, grads, 1)
    wo_in = [load_out(t, order[t]) for t in range(half_groups)]
    features_in = load(features_hbm, features, 0)
    wo_in += [load_out(t, order[t]) for t in range(half_groups, KVH)]
    wk_in = load(wk_hbm, wk, 2 + KVH)
    wv_in = load(wv_hbm, wv, 3 + KVH)
    text_in = load(text_hbm, text, 4 + KVH)

    barrier = pltpu.get_barrier_semaphore()
    for k in range(1, n_dp):
        pl.semaphore_signal(
            barrier, inc=1, device_id={"dp": lax.rem(me + k, n_dp)}, device_id_type=MESH
        )
    for k in range(1, n_mp):
        pl.semaphore_signal(
            barrier, inc=1, device_id={"mp": lax.rem(z + k, n_mp)}, device_id_type=MESH
        )

    def pair_copy(src, dst, at):
        return pltpu.make_async_remote_copy(
            src_ref=src,
            dst_ref=dst,
            send_sem=pair_send.at[at],
            recv_sem=pair_recv.at[at],
            device_id={"dp": mate},
            device_id_type=MESH,
        )

    first_row = me * tok
    ends = []
    running = jnp.int32(0)
    for i in range(images):
        running = running + tiles[0, i]
        ends.append(running)

    def image_at(row):
        found = jnp.int32(0)
        for end in ends:
            found = found + jnp.where(row >= end, 1, 0)
        return found

    def pick(options, index):
        chosen_one = options[0]
        for i in range(1, images):
            chosen_one = jnp.where(index == i, options[i], chosen_one)
        return chosen_one

    first = image_at(first_row)
    last = image_at(first_row + tok - 1)
    end_first = pick(ends, first)
    end_last = pick(ends, last)
    ends_here = end_first <= first_row + tok
    slot = pick([slots[0, i] for i in range(images)], first)
    slot = jnp.where(ends_here, slot, 2 * seq)
    rows_at = first_row + lax.broadcasted_iota(jnp.int32, (tok, 1), 0)
    in_first = rows_at < end_first

    for g in range(KVH):
        query_t[g] = to_cols(queries[:, g * block : (g + 1) * block].astype(F32)).astype(BF16)

    grads_in.wait()
    take = (
        lax.broadcasted_iota(jnp.int32, (lat, seq), 0) + slot
        == lax.broadcasted_iota(jnp.int32, (lat, seq), 1)
    )
    taken = dot(jnp.where(take, 1.0, 0.0).astype(BF16), grads[0]).astype(BF16)

    def upstream(t):
        wo_in[t].wait()
        up = lax.dot_general(
            taken,
            wo[pl.ds(pl.multiple_of(order[t] * block, block), block), :],
            (((1,), (1,)), ((), ())),
            preferred_element_type=F32,
        )
        owner = 1 - core if t < half_groups else core
        u_own[owner, pl.ds((t % half_groups) * HEAD, HEAD), :] = to_cols(up).astype(BF16)

    for t in range(half_groups):
        upstream(t)
    pl.semaphore_wait(barrier, n_dp + n_mp - 2)
    u_pair = pair_copy(u_own.at[1 - core], u_recv, 0)
    u_pair.start()
    for t in range(half_groups, KVH):
        upstream(t)
    u_gather = Gather(chips, chip, core, lambda j, c: u_all.at[j, c], u_send, u_got)
    u_pair.wait()
    u_all[chip, core] = u_own[core] + u_recv[...]
    u_gather.start()

    features_in.wait()
    wide = features[0].astype(F32)
    mean_square = jnp.mean(wide * wide, axis=-1, keepdims=True)
    features[0] = (wide * lax.rsqrt(mean_square + epsilon) * gain[...]).astype(BF16)

    wk_in.wait()
    projected_keys = dot(features[0], wk[...])
    keys_t[...] = projected_keys.T.astype(BF16)
    for g in range(KVH):
        keys[g] = projected_keys[:, g * HEAD : (g + 1) * HEAD].astype(BF16)
    wv_in.wait()
    projected_values = dot(features[0], wv[...])
    values_t[...] = projected_values.T.astype(BF16)
    for g in range(KVH):
        values[g] = projected_values[:, g * HEAD : (g + 1) * HEAD].astype(BF16)

    peaks, totals = ([[], []], [[], []])
    for g in range(KVH):
        scores = dot(keys[g], query_t[g]) * scale
        peak_first = jnp.max(jnp.where(in_first, scores, LOW), axis=0, keepdims=True)
        peak_last = jnp.max(jnp.where(in_first, LOW, scores), axis=0, keepdims=True)
        weight = jnp.exp(scores - jnp.where(in_first, peak_first, peak_last))
        weights[g] = weight
        weight_first = jnp.where(in_first, weight, 0.0)
        weight_last = jnp.where(in_first, 0.0, weight)
        peaks[0].append(peak_first)
        peaks[1].append(peak_last)
        totals[0].append(jnp.sum(weight_first, axis=0, keepdims=True))
        totals[1].append(jnp.sum(weight_last, axis=0, keepdims=True))
        value_cols = values_t[pl.ds(g * HEAD, HEAD), :]
        sums[0, g] = dot(value_cols, weight_first.astype(BF16))
        sums[1, g] = dot(value_cols, weight_last.astype(BF16))

    def to_all(ref, send, recv):
        return Direct(
            chips, chip, core, lambda j, c: ref.at[chip, core], lambda j, c: ref.at[j, c], send, recv
        )

    stats[chip, core] = jnp.concatenate(peaks[0] + totals[0] + peaks[1] + totals[1], axis=0)
    s_gather = to_all(stats, s_send, s_got)
    s_gather.all_start()
    u_gather.forward()
    s_gather.finish()

    own = stats[chip, core]
    parts = []
    for d in range(n_dp):
        got = stats[d // 2, d % 2]
        for part, image in enumerate((image_at(d * tok), image_at(d * tok + tok - 1))):
            at = 2 * KVH * part
            parts.append((image, got[at : at + KVH], got[at + KVH : at + 2 * KVH]))

    def whole(mine, local_peak):
        peak = jnp.full_like(local_peak, LOW)
        for image, part_peak, _ in parts:
            peak = jnp.maximum(peak, jnp.where(image == mine, part_peak, LOW))
        total = jnp.zeros_like(peak)
        for image, part_peak, part_total in parts:
            share = part_total * jnp.exp(part_peak - peak)
            total = total + jnp.where(image == mine, share, 0.0)
        return jnp.exp(local_peak - peak) / total

    factors = (whole(first, own[0:KVH]), whole(last, own[2 * KVH : 3 * KVH]))
    for part in range(2):
        for g in range(KVH):
            rescale[part, g] = factors[part][g : g + 1]
            sums[part, g] = sums[part, g] * factors[part][g : g + 1]
    u_gather.finish()

    chip_first = lax.div(end_first - 1, 2 * tok)
    chip_last = lax.div(end_last - 1, 2 * tok)

    def up_of(where_from, g):
        at = g * HEAD
        return u_all[where_from, at // half, pl.ds(at % half, HEAD), :]

    dots[chip, core] = jnp.concatenate(
        [
            jnp.sum(up_of(where_from, g).astype(F32) * sums[part, g], axis=0, keepdims=True)
            for part, where_from in enumerate((chip_first, chip_last))
            for g in range(KVH)
        ],
        axis=0,
    )
    d_gather = to_all(dots, d_send, d_got)
    d_gather.all_start()
    for g in range(KVH):
        dot_first = dot(values[g], up_of(chip_first, g))
        dot_last = dot(values[g], up_of(chip_last, g))
        chosen[g] = jnp.where(in_first, dot_first, dot_last)
        weights[g] = weights[g] * jnp.where(in_first, rescale[0, g], rescale[1, g])
    d_gather.finish()

    inner_first = jnp.zeros((KVH, dots.shape[3]), F32)
    inner_last = inner_first
    for d in range(n_dp):
        got = dots[d // 2, d % 2]
        for part, image in enumerate((image_at(d * tok), image_at(d * tok + tok - 1))):
            piece = got[part * KVH : (part + 1) * KVH]
            inner_first = inner_first + jnp.where(image == first, piece, 0.0)
            inner_last = inner_last + jnp.where(image == last, piece, 0.0)
    for g in range(KVH):
        rescale[0, g] = inner_first[g : g + 1]
        rescale[1, g] = inner_last[g : g + 1]

    g_rows = g_own.shape[2]
    per_group = chips // KVH
    g_scatter = Direct(
        chips,
        chip,
        core,
        lambda j, c: g_own.at[c, j],
        lambda j, c: g_chip.at[j, c],
        gc_send,
        gc_got,
    )
    my_group = lax.div(chip, per_group)
    for t in (1, 3, 2, 0):
        g = lax.rem(my_group + t, KVH)
        inner = jnp.where(in_first, rescale[0, g], rescale[1, g])
        grad = weights[g] * (chosen[g] - inner)
        cols_t = keys_t[pl.ds(pl.multiple_of(g * HEAD, HEAD), HEAD), :]
        term = (dot(cols_t, grad.astype(BF16)) * scale)
        lanes = term.shape[1] // 2
        for p in range(per_group):
            for c in range(2):
                g_own[c, g * per_group + p] = term[
                    p * g_rows : (p + 1) * g_rows, c * lanes : (c + 1) * lanes
                ].astype(BF16)
        if per_group == 1:
            for q in range(2):
                if t or q:
                    g_scatter.start(t, q)
    if per_group != 1:
        g_scatter.all_start()

    for g in range(KVH):
        share_first = sums[0, g]
        share_last = sums[1, g]
        for i in range(images):
            share = jnp.where(first == i, share_first, 0.0) + jnp.where(last == i, share_last, 0.0)
            at = g * HEAD
            a_own[at // half, pl.ds(i * half + at % half, HEAD), :] = share.astype(BF16)
    a_pair_copy = pair_copy(a_own.at[1 - core], a_recv, 2)
    a_pair_copy.start()

    def scatter(src, rows, dst, send, recv, k, target_chip):
        return pltpu.make_async_remote_copy(
            src_ref=src.at[pl.ds(pl.multiple_of(target_chip * rows, rows), rows)],
            dst_ref=dst.at[k],
            send_sem=send.at[k],
            recv_sem=recv.at[k],
            device_id={"dp": target_chip * 2 + core},
            device_id_type=MESH,
        )

    a_rows = a_pair.shape[0] // chips
    a_pair_copy.wait()
    a_pair[...] = (a_own[core].astype(F32) + a_recv[...].astype(F32)).astype(BF16)
    a_scatter = [
        scatter(a_pair, a_rows, a_chip, ac_send, ac_got, k, lax.rem(chip + k, chips))
        for k in range(1, chips)
    ]
    for copy in a_scatter:
        copy.start()

    g_chip[chip, core] = g_own[core, chip]
    g_scatter.finish()
    g_piece = g_chip[0, 0].astype(F32)
    for d in range(1, n_dp):
        g_piece = g_piece + g_chip[d // 2, d % 2].astype(F32)
    z_all[z] = g_piece
    z_copies = [
        pltpu.make_async_remote_copy(
            src_ref=z_all.at[z],
            dst_ref=z_all.at[z],
            send_sem=z_send.at[k],
            recv_sem=z_got.at[k],
            device_id={"mp": lax.rem(z + k, n_mp)},
            device_id_type=MESH,
        )
        for k in range(1, n_mp)
    ]
    for copy in z_copies:
        copy.start()

    for copy in a_scatter:
        copy.wait()
    a_piece = a_pair[pl.ds(pl.multiple_of(chip * a_rows, a_rows), a_rows), :].astype(F32)
    for k in range(1, chips):
        a_piece = a_piece + a_chip[k].astype(F32)
    a_all[core, pl.ds(pl.multiple_of(chip * a_rows, a_rows), a_rows), :] = a_piece.astype(BF16)
    a_gather = Gather(
        chips,
        chip,
        core,
        lambda j, c: a_all.at[c, pl.ds(pl.multiple_of(j * a_rows, a_rows), a_rows)],
        a_send,
        a_got,
    )
    a_gather.start()

    for k in range(1, n_mp):
        origin = lax.rem(z + n_mp - k, n_mp)
        pltpu.make_async_remote_copy(
            src_ref=z_all.at[origin],
            dst_ref=z_all.at[origin],
            send_sem=z_send.at[k],
            recv_sem=z_got.at[k],
            device_id={"mp": origin},
            device_id_type=MESH,
        ).wait_recv()
    g_sum = z_all[0]
    for k in range(1, n_mp):
        g_sum = g_sum + z_all[k]
    g_all[chip, core] = g_sum.astype(BF16)
    g_gather = to_all(g_all, g_send, g_got)
    g_gather.all_start()
    for copy in z_copies:
        copy.wait_send()

    a_gather.forward()
    a_gather.finish()
    halves = []
    for part in range(2):
        attended = a_all[part, 0:half, :].astype(F32)
        for i in range(1, images):
            other = a_all[part, i * half : (i + 1) * half, :].astype(F32)
            attended = jnp.where(first == i, other, attended)
        halves.append(attended)
    attended_rows = to_rows(jnp.concatenate(halves, axis=0), lat).astype(BF16)
    put = (
        lax.broadcasted_iota(jnp.int32, (seq, lat), 1) + slot
        == lax.broadcasted_iota(jnp.int32, (seq, lat), 0)
    )
    shifted = dot(jnp.where(put, 1.0, 0.0).astype(BF16), attended_rows).astype(BF16)
    row_at = lax.broadcasted_iota(jnp.int32, (seq, 1), 0)
    inside = (row_at >= slot) & (row_at < slot + lat)
    text_in.wait()
    projected = dot(shifted, wo[...]).astype(BF16)
    merged[0] = jnp.where(inside, projected.astype(F32), text[0].astype(F32)).astype(BF16)

    g_gather.finish()
    whole_rows = [
        jnp.concatenate([g_all[j, 0].astype(F32), g_all[j, 1].astype(F32)], axis=1)
        for j in range(chips)
    ]
    query_grad[...] = to_rows(jnp.concatenate(whole_rows, axis=0), lat)


def on_device(
    n_dp, n_mp, features, context_gain, queries, w_key, w_value, w_out, image_tiles, slot_start, text_rows, row_grads
):
    _, tok, width = features.shape
    images = image_tiles.shape[1]
    lat = queries.shape[0]
    _, seq, dm = text_rows.shape
    chips = n_dp // 2
    block = KVH * HEAD
    half = block // 2
    cols = PER * lat
    a_rows = images * half // chips
    g_rows = block // chips
    gathers = pltpu.SemaphoreType.DMA((2 * chips - 1,))
    direct = pltpu.SemaphoreType.DMA((n_dp,))
    vmem = pl.BlockSpec(memory_space=pltpu.VMEM)
    smem = pl.BlockSpec(memory_space=pltpu.SMEM)
    anywhere = pl.BlockSpec(memory_space=pl.ANY)
    return pl.pallas_call(
        functools.partial(kernel, (n_dp, n_mp, images, lat, tok, seq)),
        out_shape=(
            pltpu.VMEM(text_rows.shape, BF16),
            pltpu.VMEM(queries.shape, F32),
        ),
        in_specs=[smem, smem, vmem, vmem] + [anywhere] * 6,
        out_specs=(vmem, vmem),
        scratch_shapes=[
            pltpu.VMEM(features.shape, BF16),
            pltpu.VMEM(w_key.shape, BF16),
            pltpu.VMEM(w_value.shape, BF16),
            pltpu.VMEM(w_out.shape, BF16),
            pltpu.VMEM(text_rows.shape, BF16),
            pltpu.VMEM(row_grads.shape, BF16),
            pltpu.VMEM((KVH, tok, HEAD), BF16),
            pltpu.VMEM((KVH, tok, HEAD), BF16),
            pltpu.VMEM((block, tok), BF16),
            pltpu.VMEM((block, tok), BF16),
            pltpu.VMEM((KVH, HEAD, cols), BF16),
            pltpu.VMEM((KVH, tok, cols), F32),
            pltpu.VMEM((KVH, tok, cols), F32),
            pltpu.VMEM((2, KVH, HEAD, cols), F32),
            pltpu.VMEM((2, half, cols), BF16),
            pltpu.VMEM((half, cols), BF16),
            pltpu.VMEM((chips, 2, half, cols), BF16),
            pltpu.VMEM((chips, 2, 4 * KVH, cols), F32),
            pltpu.VMEM((chips, 2, 2 * KVH, cols), F32),
            pltpu.VMEM((2, KVH, 1, cols), F32),
            pltpu.VMEM((2, chips, g_rows, cols // 2), BF16),
            pltpu.VMEM((chips, 2, g_rows, cols // 2), BF16),
            pltpu.VMEM((n_mp, g_rows, cols // 2), F32),
            pltpu.VMEM((chips, 2, g_rows, cols // 2), BF16),
            pltpu.VMEM((2, images * half, cols), BF16),
            pltpu.VMEM((images * half, cols), BF16),
            pltpu.VMEM((images * half, cols), BF16),
            pltpu.VMEM((chips, a_rows, cols), BF16),
            pltpu.VMEM((2, images * half, cols), BF16),
            pltpu.SemaphoreType.DMA((5 + KVH,)),
            pltpu.SemaphoreType.DMA((3,)),
            pltpu.SemaphoreType.DMA((3,)),
            gathers,
            gathers,
            direct,
            direct,
            direct,
            direct,
            direct,
            direct,
            pltpu.SemaphoreType.DMA((n_mp,)),
            pltpu.SemaphoreType.DMA((n_mp,)),
            direct,
            direct,
            pltpu.SemaphoreType.DMA((chips,)),
            pltpu.SemaphoreType.DMA((chips,)),
            gathers,
            gathers,
        ],
        compiler_params=pltpu.CompilerParams(
            collective_id=0, has_side_effects=True, vmem_limit_bytes=60 * 1024 * 1024
        ),
        name="resampler",
    )(
        image_tiles,
        slot_start,
        context_gain,
        queries,
        features,
        w_key,
        w_value,
        w_out,
        text_rows,
        row_grads,
    )


def solution(mesh):
    placed = (
        P("mp", "dp", None),
        P(),
        P(),
        P(),
        P(),
        P(),
        P("mp", None),
        P("mp", None),
        P("mp", "dp", None),
        P("mp", "dp", None),
    )
    return jax.shard_map(
        functools.partial(on_device, mesh.shape["dp"], mesh.shape["mp"]),
        mesh=mesh,
        in_specs=placed,
        out_specs=(P("mp", "dp", None), P()),
        check_vma=False,
    )
```

profile of v0, /device:TPU:0, one launch (start us, length us, event | category | flops | bytes accessed | tf_op | source)
XLA Modules:
  0.0 38.0 jit_solution(3219167862508395782)
XLA Ops:
  0.6 35.8 %resampler.1 = (bf16[1,128,2048]{2,1,0:T(8,128)(2,1)S(1)}, f32[64,1536]{1,0:T(8,128)S(1)}) custom-call(s32[1,2]{1,0:T(1,128)} %tiles.1, s32[1,2]{1,0:T(1,128)} %slots.1, f32[1152]{0:T(1024)} %gain.1, bf16[64,1536]{1,0:T(8,128)(2,1)} %queries.1, bf16[1,512,1152]{2,1,0:T(8,128)(2,1)} %features_hbm.1, bf16[1152,384]{1,0:T(8,128)(2,1)} %wk_hbm.1, ...), custom_call_target="tpu_custom_call" | custom-call | tf_op jit(solution)/shard_map/resampler/pallas_call | solution.py:573
  36.5 0.8 %copy.14 = bf16[1,128,2048]{2,1,0:T(8,128)(2,1)} copy(bf16[1,128,2048]{2,1,0:T(8,128)(2,1)S(1)} %get-tuple-element.2) | data formatting | bytes 1048576
  37.3 0.7 %copy.15 = f32[64,1536]{1,0:T(8,128)} copy(f32[64,1536]{1,0:T(8,128)S(1)} %get-tuple-element.3) | data formatting | bytes 786432
where the time goes:
time: 38.2 us; the launch traced here: 38 us
  Pallas kernels  35.8 us (94%)
  local copies, waits for them, and re-layouts  1.54 us (4%)
  between operations  0.64 us (2%)
    pallas_call x1, Pallas kernels, on_device(): pl.pallas_call(functools.partial(kernel, (n_dp, n_mp, images, lat, tok, s...  35.8 us
    unnamed x2, local copies, waits for them, and re-layouts  1.54 us

commit v1 on v0

v1 whole, which is shorter than its diff:
```python
import functools

import jax
import jax.numpy as jnp
from jax import lax
from jax.experimental import pallas as pl
from jax.experimental.pallas import tpu as pltpu
from jax.sharding import PartitionSpec as P

HEADS = 16
HEAD = 96
KVH = 4
PER = HEADS // KVH
CORES = 2
HALF = KVH // CORES
LANES = 128
epsilon = 1e-06
LOW = -1e30
MESH = pl.DeviceIdType.MESH
F32 = jnp.float32
BF16 = jnp.bfloat16


def to_cols(rows):
    stacked = jnp.concatenate([rows[:, c * HEAD : (c + 1) * HEAD] for c in range(PER)], axis=0)
    return stacked.T


def to_rows(cols, lat):
    flipped = cols.T
    return jnp.concatenate(
        [
            flipped[c * lat : (c + 1) * lat, g * HEAD : (g + 1) * HEAD]
            for g in range(cols.shape[0] // HEAD)
            for c in range(PER)
        ],
        axis=1,
    )


def dot(a, b):
    return jnp.dot(a, b, preferred_element_type=F32)


def remote(src, dst, send, recv, **to):
    return pltpu.make_async_remote_copy(
        src_ref=src, dst_ref=dst, send_sem=send, recv_sem=recv, device_id=to, device_id_type=MESH
    )


class Spread:
    def __init__(self, chips, chip, core, src, dst, send, recv):
        self.chips, self.chip, self.core = chips, chip, core
        self.src, self.dst, self.send, self.recv = src, dst, send, recv

    def hop(self, k, src_chip, dst_chip, target):
        return remote(
            self.src(src_chip), self.dst(dst_chip), self.send.at[k], self.recv.at[k], dp=target * CORES + self.core
        )

    def start(self):
        for k in range(1, self.chips):
            there = lax.rem(self.chip + k, self.chips)
            self.hop(k, there, self.chip, there).start()

    def wait(self):
        for k in range(1, self.chips):
            origin = lax.rem(self.chip + self.chips - k, self.chips)
            self.hop(k, origin, origin, origin).wait_recv()

    def drain(self):
        for k in range(1, self.chips):
            there = lax.rem(self.chip + k, self.chips)
            self.hop(k, there, self.chip, there).wait_send()


def kernel(
    dims,
    tiles_hbm,
    slots_hbm,
    gain_hbm,
    queries_hbm,
    features_hbm,
    wk_hbm,
    wv_hbm,
    wo_hbm,
    text_hbm,
    grads_hbm,
    merged,
    query_grad,
    tiles,
    slots,
    gain,
    queries,
    features,
    wkv,
    wo,
    text,
    grads,
    taken,
    both,
    kv_out,
    kv_rows,
    lhs,
    query_t,
    weights,
    sums,
    g_one,
    u_all,
    u_pair,
    stats,
    a_own,
    a_raw,
    a_all,
    att,
    g_own,
    g_chip,
    z_all,
    g_all,
    load_sem,
    pair_send,
    pair_recv,
    u_send,
    u_got,
    s_send,
    s_got,
    ar_send,
    ar_got,
    ag_send,
    ag_got,
    gr_send,
    gr_got,
    z_send,
    z_got,
    gg_send,
    gg_got,
):
    n_dp, n_mp, images, lat, tok, seq = dims
    chips = n_dp // CORES
    me = lax.axis_index("dp")
    z = lax.axis_index("mp")
    chip = lax.div(me, CORES)
    core = lax.rem(me, CORES)
    mate = chip * CORES + 1 - core
    scale = HEAD ** (-0.5)
    block = PER * HEAD
    wide_half = HALF * block
    split = HALF * HEAD

    def load(src, dst, at):
        copy = pltpu.make_async_copy(src, dst, load_sem.at[at])
        copy.start()
        return copy

    def half_rows(c):
        return pl.ds(pl.multiple_of(c * wide_half, wide_half), wide_half)

    tiles_in = load(tiles_hbm, tiles, 9)
    slots_in = load(slots_hbm, slots, 10)
    grads_in = load(grads_hbm, grads, 0)
    features_in = load(features_hbm, features, 1)
    gain_in = load(gain_hbm, gain, 2)
    wk_in = load(wk_hbm, wkv.at[:, pl.ds(0, KVH * HEAD)], 3)
    wo_near = load(wo_hbm.at[half_rows(core)], wo.at[half_rows(core)], 5)
    wv_in = load(wv_hbm, wkv.at[:, pl.ds(KVH * HEAD, KVH * HEAD)], 4)
    queries_in = load(queries_hbm.at[:, half_rows(core)], queries, 6)
    wo_far = load(wo_hbm.at[half_rows(1 - core)], wo.at[half_rows(1 - core)], 7)
    text_in = load(text_hbm, text, 8)

    barrier = pltpu.get_barrier_semaphore()
    for k in range(1, n_dp):
        pl.semaphore_signal(
            barrier, inc=1, device_id={"dp": lax.rem(me + k, n_dp)}, device_id_type=MESH
        )
    for k in range(1, n_mp):
        pl.semaphore_signal(
            barrier, inc=1, device_id={"mp": lax.rem(z + k, n_mp)}, device_id_type=MESH
        )

    tiles_in.wait()
    slots_in.wait()
    ends = []
    running = jnp.int32(0)
    for i in range(images):
        running = running + tiles[0, i]
        ends.append(running)

    def image_at(row):
        found = jnp.int32(0)
        for end in ends:
            found = found + jnp.where(row >= end, 1, 0)
        return found

    def pick(options, index):
        chosen_one = options[0]
        for i in range(1, images):
            chosen_one = jnp.where(index == i, options[i], chosen_one)
        return chosen_one

    own_image = image_at(me * tok)
    ends_here = pick(ends, own_image) <= (me + 1) * tok
    slot = pick([slots[0, i] for i in range(images)], own_image)
    slot = jnp.where(ends_here, slot, 2 * seq)

    chip_rows = CORES * tok
    spans = [(image_at(d * chip_rows), image_at((d + 1) * chip_rows - 1)) for d in range(chips)]
    first_row = chip * chip_rows
    first = image_at(first_row)
    last = image_at(first_row + chip_rows - 1)
    end_first = pick(ends, first)
    end_last = pick(ends, last)
    chip_first = lax.div(end_first - 1, chip_rows)
    chip_last = lax.div(end_last - 1, chip_rows)
    in_first = [
        first_row + s * tok + lax.broadcasted_iota(jnp.int32, (tok, 1), 0) < end_first for s in range(CORES)
    ]

    grads_in.wait()
    take = (
        lax.broadcasted_iota(jnp.int32, (lat, seq), 0) + slot
        == lax.broadcasted_iota(jnp.int32, (lat, seq), 1)
    )
    taken[core] = dot(jnp.where(take, 1.0, 0.0).astype(BF16), grads[0]).astype(BF16)
    pl.semaphore_wait(barrier, n_dp + n_mp - 2)
    taken_out = remote(taken.at[core], taken.at[core], pair_send.at[0], pair_recv.at[0], dp=mate)
    taken_out.start()

    features_in.wait()
    gain_in.wait()
    wide = features[0].astype(F32)
    mean_square = jnp.mean(wide * wide, axis=-1, keepdims=True)
    features[0] = (wide * lax.rsqrt(mean_square + epsilon) * gain[...]).astype(BF16)
    wk_in.wait()
    early = 2 * LANES
    both[:, 0:early] = dot(features[0], wkv[:, 0:early]).astype(BF16)

    remote(taken.at[1 - core], taken.at[1 - core], pair_send.at[0], pair_recv.at[0], dp=mate).wait_recv()
    wo_near.wait()
    flipped = (taken[0] + taken[1]).T
    u_spread = []
    for t in range(HALF):
        at = pl.multiple_of((core * HALF + t) * block, block)
        up = dot(wo[pl.ds(at, block), :], flipped)
        u_all[t][chip] = jnp.concatenate(
            [up[c * HEAD : (c + 1) * HEAD] for c in range(PER)], axis=1
        ).astype(BF16)
        u_spread.append(
            Spread(
                chips, chip, core,
                lambda j, t=t: u_all[t].at[chip], lambda j, t=t: u_all[t].at[j],
                u_send.at[t], u_got.at[t],
            )
        )
        u_spread[t].start()
    wv_in.wait()
    both[:, early:] = dot(features[0], wkv[:, early:]).astype(BF16)
    pad = jnp.zeros((tok, LANES - HEAD), BF16)

    def columns(kind, g):
        at = kind * KVH * HEAD + g * HEAD
        return jnp.concatenate([both[:, at : at + HEAD], pad], axis=1)

    for c in range(CORES):

        @pl.when(core == c)
        def _():
            for kind in range(2):
                for t in range(HALF):
                    kv_out[kind, t] = columns(kind, (1 - c) * HALF + t)
                    kv_rows[c, kind, t] = columns(kind, c * HALF + t)

    kv_copy = remote(kv_out, kv_rows.at[core], pair_send.at[1], pair_recv.at[1], dp=mate)
    kv_copy.start()
    queries_in.wait()
    for t in range(HALF):
        query_t[t, 0:HEAD] = to_cols(queries[:, t * block : (t + 1) * block].astype(F32)).astype(BF16)
        query_t[t, HEAD:LANES] = jnp.zeros((LANES - HEAD, query_t.shape[2]), BF16)

    def flip(s):
        lane = first_row + s * tok + lax.broadcasted_iota(jnp.int32, (HEAD, tok), 1)
        keep = jnp.where(lane < end_first, 1.0, 0.0).astype(BF16)
        for t in range(HALF):
            for kind in range(2):
                cols = kv_rows[s, 1 - kind, t].T[0:HEAD]
                kept = cols * keep
                at = kind * 2 * HEAD
                lhs[s, t, at : at + HEAD] = kept
                lhs[s, t, at + HEAD : at + 2 * HEAD] = cols - kept

    flip(core)
    remote(kv_out, kv_rows.at[1 - core], pair_send.at[1], pair_recv.at[1], dp=mate).wait_recv()
    flip(1 - core)

    peaks, totals = [], []
    for t in range(HALF):
        scores = [dot(kv_rows[s, 0, t], query_t[t]) for s in range(CORES)]
        peak = [
            functools.reduce(
                jnp.maximum,
                [
                    jnp.max(
                        jnp.where(in_first[s], scores[s], LOW) if q == 0 else jnp.where(in_first[s], LOW, scores[s]),
                        axis=0, keepdims=True,
                    )
                    for s in range(CORES)
                ],
            )
            for q in range(2)
        ]
        total = [0.0, 0.0]
        product = 0.0
        for s in range(CORES):
            weight = jnp.exp((scores[s] - jnp.where(in_first[s], peak[0], peak[1])) * scale)
            weights[t, s] = weight
            total[0] = total[0] + jnp.sum(jnp.where(in_first[s], weight, 0.0), axis=0, keepdims=True)
            total[1] = total[1] + jnp.sum(jnp.where(in_first[s], 0.0, weight), axis=0, keepdims=True)
            product = product + dot(lhs[s, t], weight.astype(BF16))
        sums[t] = product
        peaks.append([p * scale for p in peak])
        totals.append(total)

    share = split // chips
    for j in range(chips):
        t, at = divmod(j * share, HEAD)
        for q in range(2):
            a_own[j, q] = sums[t, q * HEAD + at : q * HEAD + at + share].astype(BF16)
    raw_spread = Spread(chips, chip, core, lambda j: a_own.at[j], lambda j: a_raw.at[j], ar_send, ar_got)
    s_spread, local = [], []
    for t in range(HALF):
        u_spread[t].wait()
        u_pair[t, HEAD:LANES] = jnp.zeros((LANES - HEAD, u_pair.shape[2]), BF16)
        u_pair[t, LANES + HEAD : 2 * LANES] = jnp.zeros((LANES - HEAD, u_pair.shape[2]), BF16)
        rows_here, inner_here = [], []
        for q, source in enumerate((chip_first, chip_last)):
            part = u_all[t][source]
            u_pair[t, q * LANES : q * LANES + HEAD] = part
            d = jnp.sum(part.astype(F32) * sums[t, q * HEAD : (q + 1) * HEAD], axis=0, keepdims=True)
            rows_here += [peaks[t][q], totals[t][q], d]
            inner_here.append(d / jnp.maximum(totals[t][q], 1.0))
        stats[t, chip] = jnp.concatenate(rows_here + [jnp.zeros_like(d)] * 2, axis=0)
        s_spread.append(
            Spread(
                chips, chip, core,
                lambda j, t=t: stats.at[t, chip], lambda j, t=t: stats.at[t, j],
                s_send.at[t], s_got.at[t],
            )
        )
        s_spread[t].start()
        local.append(inner_here)
    raw_spread.start()

    for t in range(HALF):
        one = 0.0
        for s in range(CORES):
            value = kv_rows[s, 1, t]
            row = first_row + s * tok + lax.broadcasted_iota(jnp.int32, (tok, LANES), 0)
            kept = value * jnp.where(row < end_first, 1.0, 0.0).astype(BF16)
            chosen = dot(jnp.concatenate([kept, value - kept], axis=1), u_pair[t])
            grad = weights[t, s] * (chosen - jnp.where(in_first[s], local[t][0], local[t][1]))
            one = one + dot(lhs[s, t, 2 * HEAD : 4 * HEAD], grad.astype(BF16))
        g_one[t] = one

    def whole(got, mine):
        peak = jnp.full_like(got[0][0:1], LOW)
        for d in range(chips):
            for q in range(2):
                peak = jnp.maximum(peak, jnp.where(spans[d][q] == mine, got[d][3 * q : 3 * q + 1], LOW))
        shares, total, inner = [], 0.0, 0.0
        for d in range(chips):
            for q in range(2):
                share_of = jnp.where(
                    spans[d][q] == mine, jnp.exp(got[d][3 * q : 3 * q + 1] - peak), 0.0
                )
                shares.append(share_of)
                total = total + share_of * got[d][3 * q + 1 : 3 * q + 2]
                inner = inner + share_of * got[d][3 * q + 2 : 3 * q + 3]
        return peak, shares, total, inner

    g_rows = HEAD // chips
    g_spread = []
    for t in range(HALF):
        s_spread[t].wait()
        got = [stats[t, d] for d in range(chips)]
        term = 0.0
        for q, mine in enumerate((first, last)):
            peak, _, total, inner = whole(got, mine)
            factor = jnp.exp(peaks[t][q] - peak) / total * scale
            shift = inner / total - local[t][q]
            at = q * HEAD
            term = term + factor * (
                g_one[t, at : at + HEAD] - shift * sums[t, 2 * HEAD + at : 2 * HEAD + at + HEAD]
            )
        for j in range(chips):
            g_own[t, j] = term[j * g_rows : (j + 1) * g_rows].astype(BF16)
        g_spread.append(
            Spread(
                chips, chip, core,
                lambda j, t=t: g_own.at[t, j], lambda j, t=t: g_chip.at[t, j],
                gr_send.at[t], gr_got.at[t],
            )
        )
        g_spread[t].start()

    raw_spread.wait()
    a_raw[chip] = a_own[chip]
    group = lax.div(chip, chips // HALF)
    got = [stats[group, d] for d in range(chips)]
    for i in range(images):
        _, shares, total, _ = whole(got, i)
        acc = 0.0
        for d in range(chips):
            for q in range(2):
                acc = acc + shares[2 * d + q] * a_raw[d, q].astype(F32)
        a_all[chip, i] = (acc / total).astype(BF16)
    a_spread = Spread(chips, chip, core, lambda j: a_all.at[chip], lambda j: a_all.at[j], ag_send, ag_got)
    a_spread.start()

    def z_hop(t, k, at, target):
        return remote(z_all.at[t, at], z_all.at[t, at], z_send.at[t, k], z_got.at[t, k], mp=target)

    for t in range(HALF):
        g_spread[t].wait()
        piece = g_own[t, chip].astype(F32)
        for k in range(1, chips):
            piece = piece + g_chip[t, lax.rem(chip + k, chips)].astype(F32)
        z_all[t, z] = piece.astype(BF16)
        for k in range(1, n_mp):
            z_hop(t, k, z, lax.rem(z + k, n_mp)).start()

    def g_hop(t, k, q, origin, target):
        ref = g_all.at[t, origin[1], origin[0]]
        at = CORES * k + q
        return remote(ref, ref, gg_send.at[t, at], gg_got.at[t, at], dp=target[0] * CORES + target[1])

    def other(k, q):
        return (lax.rem(chip + k, chips), 1 - core if q else core)

    hops = [(k, q) for k in list(range(1, chips)) + [0] for q in range(CORES) if k or q]
    def pick_attended():
        a_spread.wait()
        picked = jnp.concatenate([a_all[j, 0].astype(F32) for j in range(chips)], axis=0)
        for i in range(1, images):
            option = jnp.concatenate([a_all[j, i].astype(F32) for j in range(chips)], axis=0)
            picked = jnp.where(first == i, option, picked)
        att[core] = picked.astype(BF16)
        att_copy = remote(att.at[core], att.at[core], pair_send.at[2], pair_recv.at[2], dp=mate)
        att_copy.start()
        return att_copy

    for t in range(HALF):
        for k in range(1, n_mp):
            origin = lax.rem(z + n_mp - k, n_mp)
            z_hop(t, k, origin, origin).wait_recv()
        g_sum = z_all[t, 0].astype(F32)
        for k in range(1, n_mp):
            g_sum = g_sum + z_all[t, k].astype(F32)
        g_all[t, core, chip] = g_sum.astype(BF16)
        for k, q in hops:
            g_hop(t, k, q, (chip, core), other(k, q)).start()
        if t == 0:
            att_copy = pick_attended()

    wo_far.wait()
    text_in.wait()
    put = (
        lax.broadcasted_iota(jnp.int32, (seq, lat), 1) + slot
        == lax.broadcasted_iota(jnp.int32, (seq, lat), 0)
    )
    put = jnp.where(put, 1.0, 0.0).astype(BF16)

    def project(c):
        placed = dot(put, to_rows(att[c].astype(F32), lat).astype(BF16)).astype(BF16)
        return dot(placed, wo[half_rows(c), :])

    near = project(core)
    remote(att.at[1 - core], att.at[1 - core], pair_send.at[2], pair_recv.at[2], dp=mate).wait_recv()
    projected = (near + project(1 - core)).astype(BF16)
    row_at = lax.broadcasted_iota(jnp.int32, (seq, 1), 0)
    inside = (row_at >= slot) & (row_at < slot + lat)
    merged[0] = jnp.where(inside, projected.astype(F32), text[0].astype(F32)).astype(BF16)

    for t in range(HALF):
        for k, q in hops:
            origin = other(chips - k, q)
            g_hop(t, k, q, origin, origin).wait_recv()
    cols = jnp.concatenate(
        [g_all[t, c, j].astype(F32) for c in range(CORES) for t in range(HALF) for j in range(chips)], axis=0
    )
    query_grad[...] = to_rows(cols, lat)
    for copy in (taken_out, kv_copy, att_copy):
        copy.wait_send()
    for spread in u_spread + s_spread + g_spread + [raw_spread, a_spread]:
        spread.drain()
    for t in range(HALF):
        for k in range(1, n_mp):
            z_hop(t, k, z, lax.rem(z + k, n_mp)).wait_send()
        for k, q in hops:
            g_hop(t, k, q, (chip, core), other(k, q)).wait_send()


def on_device(
    n_dp, n_mp, features, context_gain, queries, w_key, w_value, w_out, image_tiles, slot_start, text_rows, row_grads
):
    _, tok, width = features.shape
    images = image_tiles.shape[1]
    lat = queries.shape[0]
    _, seq, dm = text_rows.shape
    chips = n_dp // CORES
    cols = PER * lat
    split = HALF * HEAD
    share = split // chips
    g_rows = HEAD // chips
    dma = pltpu.SemaphoreType.DMA
    vmem = pl.BlockSpec(memory_space=pltpu.VMEM)
    anywhere = pl.BlockSpec(memory_space=pl.ANY)
    return pl.pallas_call(
        functools.partial(kernel, (n_dp, n_mp, images, lat, tok, seq)),
        out_shape=(
            pltpu.VMEM(text_rows.shape, BF16),
            pltpu.VMEM(queries.shape, F32),
        ),
        in_specs=[anywhere] * 10,
        out_specs=(vmem, vmem),
        scratch_shapes=[
            pltpu.SMEM(image_tiles.shape, jnp.int32),
            pltpu.SMEM(slot_start.shape, jnp.int32),
            pltpu.VMEM(context_gain.shape, F32),
            pltpu.VMEM((lat, HALF * PER * HEAD), BF16),
            pltpu.VMEM(features.shape, BF16),
            pltpu.VMEM((width, 2 * KVH * HEAD), BF16),
            pltpu.VMEM(w_out.shape, BF16),
            pltpu.VMEM(text_rows.shape, BF16),
            pltpu.VMEM(row_grads.shape, BF16),
            pltpu.VMEM((CORES, lat, dm), BF16),
            pltpu.VMEM((tok, 2 * KVH * HEAD), BF16),
            pltpu.VMEM((2, HALF, tok, LANES), BF16),
            pltpu.VMEM((CORES, 2, HALF, tok, LANES), BF16),
            pltpu.VMEM((CORES, HALF, 4 * HEAD, tok), BF16),
            pltpu.VMEM((HALF, LANES, cols), BF16),
            pltpu.VMEM((HALF, CORES, tok, cols), F32),
            pltpu.VMEM((HALF, 4 * HEAD, cols), F32),
            pltpu.VMEM((HALF, 2 * HEAD, cols), F32),
            tuple(pltpu.VMEM((chips, HEAD, cols), BF16) for _ in range(HALF)),
            pltpu.VMEM((HALF, 2 * LANES, cols), BF16),
            pltpu.VMEM((HALF, chips, 8, cols), F32),
            pltpu.VMEM((chips, 2, share, cols), BF16),
            pltpu.VMEM((chips, 2, share, cols), BF16),
            pltpu.VMEM((chips, images, share, cols), BF16),
            pltpu.VMEM((CORES, split, cols), BF16),
            pltpu.VMEM((HALF, chips, g_rows, cols), BF16),
            pltpu.VMEM((HALF, chips, g_rows, cols), BF16),
            pltpu.VMEM((HALF, n_mp, g_rows, cols), BF16),
            pltpu.VMEM((HALF, CORES, chips, g_rows, cols), BF16),
            dma((11,)),
            dma((3,)),
            dma((3,)),
            dma((HALF, chips)),
            dma((HALF, chips)),
            dma((HALF, chips)),
            dma((HALF, chips)),
            dma((chips,)),
            dma((chips,)),
            dma((chips,)),
            dma((chips,)),
            dma((HALF, chips)),
            dma((HALF, chips)),
            dma((HALF, n_mp)),
            dma((HALF, n_mp)),
            dma((HALF, n_dp)),
            dma((HALF, n_dp)),
        ],
        compiler_params=pltpu.CompilerParams(
            collective_id=0, has_side_effects=True, vmem_limit_bytes=60 * 1024 * 1024
        ),
        name="resampler",
    )(
        image_tiles,
        slot_start,
        context_gain,
        queries,
        features,
        w_key,
        w_value,
        w_out,
        text_rows,
        row_grads,
    )


def solution(mesh):
    placed = (
        P("mp", "dp", None),
        P(),
        P(),
        P(),
        P(),
        P(),
        P("mp", None),
        P("mp", None),
        P("mp", "dp", None),
        P("mp", "dp", None),
    )
    return jax.shard_map(
        functools.partial(on_device, mesh.shape["dp"], mesh.shape["mp"]),
        mesh=mesh,
        in_specs=placed,
        out_specs=(P("mp", "dp", None), P()),
        check_vma=False,
    )
```

time: 38.2 us -> 32.6 us (0.85)
  Pallas kernels: 35.8 us -> 30.3 us
    pallas_call x1, Pallas kernels: 35.8 us -> 30.3 us  [on_device(): pl.pallas_call(functools.partial(kernel, (n_dp, n_mp, images, lat, tok, s...]
where the time goes in v1:
time: 32.6 us; the launch traced here: 32.4 us
  Pallas kernels  30.3 us (93%)
  local copies, waits for them, and re-layouts  1.54 us (5%)
  between operations  0.64 us (2%)
    pallas_call x1, Pallas kernels, on_device(): pl.pallas_call(functools.partial(kernel, (n_dp, n_mp, images, lat, tok, s...  30.3 us
    unnamed x2, local copies, waits for them, and re-layouts  1.54 us

profile of v1, /device:TPU:0, one launch (start us, length us, event | category | flops | bytes accessed | tf_op | source)
XLA Modules:
  0.0 32.4 jit_solution(4901175016195669452)
XLA Ops:
  0.6 30.3 %resampler.1 = (bf16[1,128,2048]{2,1,0:T(8,128)(2,1)S(1)}, f32[64,1536]{1,0:T(8,128)S(1)}) custom-call(s32[1,2]{1,0:T(1,128)} %tiles_hbm.1, s32[1,2]{1,0:T(1,128)} %slots_hbm.1, f32[1152]{0:T(1024)} %gain_hbm.1, bf16[64,1536]{1,0:T(8,128)(2,1)} %queries_hbm.1, bf16[1,512,1152]{2,1,0:T(8,128)(2,1)} %features_hbm.1, bf16[1152,384]{1,0:T(8,128)(2,1)} %wk_hbm.1, ...), custom_call_target="tpu_custom_call" | custom-call | tf_op jit(solution)/shard_map/resampler/pallas_call | solution.py:516
  30.9 0.8 %copy.14 = bf16[1,128,2048]{2,1,0:T(8,128)(2,1)} copy(bf16[1,128,2048]{2,1,0:T(8,128)(2,1)S(1)} %get-tuple-element.2) | data formatting | bytes 1048576
  31.7 0.7 %copy.15 = f32[64,1536]{1,0:T(8,128)} copy(f32[64,1536]{1,0:T(8,128)S(1)} %get-tuple-element.3) | data formatting | bytes 786432

commit v2 on v1

--- a/solution.py
+++ b/solution.py
@@ -16,6 +16,7 @@
 LANES = 128
 epsilon = 1e-06
 LOW = -1e30
+LOG2E = 1.4426950408889634
 MESH = pl.DeviceIdType.MESH
 F32 = jnp.float32
 BF16 = jnp.bfloat16
@@ -42,6 +43,11 @@
     return jnp.dot(a, b, preferred_element_type=F32)
 
 
+def dot_halves(a, b):
+    mid = a.shape[0] // 2
+    return jnp.concatenate([dot(a[:mid], b), dot(a[mid:], b)], axis=0)
+
+
 def remote(src, dst, send, recv, **to):
     return pltpu.make_async_remote_copy(
         src_ref=src, dst_ref=dst, send_sem=send, recv_sem=recv, device_id=to, device_id_type=MESH
@@ -49,29 +55,26 @@
 
 
 class Spread:
-    def __init__(self, chips, chip, core, src, dst, send, recv):
+    def __init__(self, chips, chip, core, src, dst, every, send, recv):
         self.chips, self.chip, self.core = chips, chip, core
-        self.src, self.dst, self.send, self.recv = src, dst, send, recv
-
-    def hop(self, k, src_chip, dst_chip, target):
-        return remote(
-            self.src(src_chip), self.dst(dst_chip), self.send.at[k], self.recv.at[k], dp=target * CORES + self.core
-        )
+        self.src, self.dst, self.every, self.send, self.recv = src, dst, every, send, recv
 
     def start(self):
         for k in range(1, self.chips):
             there = lax.rem(self.chip + k, self.chips)
-            self.hop(k, there, self.chip, there).start()
+            remote(
+                self.src(there), self.dst(self.chip), self.send, self.recv, dp=there * CORES + self.core
+            ).start()
+
+    def whole(self):
+        there = lax.rem(self.chip + 1, self.chips)
+        return remote(self.every, self.every, self.send, self.recv, dp=there * CORES + self.core)
 
     def wait(self):
-        for k in range(1, self.chips):
-            origin = lax.rem(self.chip + self.chips - k, self.chips)
-            self.hop(k, origin, origin, origin).wait_recv()
+        self.whole().wait_recv()
 
     def drain(self):
-        for k in range(1, self.chips):
-            there = lax.rem(self.chip + k, self.chips)
-            self.hop(k, there, self.chip, there).wait_send()
+        self.whole().wait_send()
 
 
 def kernel(
@@ -232,7 +235,7 @@
     features[0] = (wide * lax.rsqrt(mean_square + epsilon) * gain[...]).astype(BF16)
     wk_in.wait()
     early = 2 * LANES
-    both[:, 0:early] = dot(features[0], wkv[:, 0:early]).astype(BF16)
+    both[:, 0:early] = dot_halves(features[0], wkv[:, 0:early]).astype(BF16)
 
     remote(taken.at[1 - core], taken.at[1 - core], pair_send.at[0], pair_recv.at[0], dp=mate).wait_recv()
     wo_near.wait()
@@ -240,7 +243,7 @@
     u_spread = []
     for t in range(HALF):
         at = pl.multiple_of((core * HALF + t) * block, block)
-        up = dot(wo[pl.ds(at, block), :], flipped)
+        up = dot_halves(wo[pl.ds(at, block), :], flipped)
         u_all[t][chip] = jnp.concatenate(
             [up[c * HEAD : (c + 1) * HEAD] for c in range(PER)], axis=1
         ).astype(BF16)
@@ -248,12 +251,12 @@
             Spread(
                 chips, chip, core,
                 lambda j, t=t: u_all[t].at[chip], lambda j, t=t: u_all[t].at[j],
-                u_send.at[t], u_got.at[t],
+                u_all[t].at[pl.ds(0, chips - 1)], u_send.at[t], u_got.at[t],
             )
         )
         u_spread[t].start()
     wv_in.wait()
-    both[:, early:] = dot(features[0], wkv[:, early:]).astype(BF16)
+    both[:, early:] = dot_halves(features[0], wkv[:, early:]).astype(BF16)
     pad = jnp.zeros((tok, LANES - HEAD), BF16)
 
     def columns(kind, g):
@@ -267,10 +270,17 @@
             for kind in range(2):
                 for t in range(HALF):
                     kv_out[kind, t] = columns(kind, (1 - c) * HALF + t)
-                    kv_rows[c, kind, t] = columns(kind, c * HALF + t)
 
     kv_copy = remote(kv_out, kv_rows.at[core], pair_send.at[1], pair_recv.at[1], dp=mate)
     kv_copy.start()
+    for c in range(CORES):
+
+        @pl.when(core == c)
+        def _():
+            for kind in range(2):
+                for t in range(HALF):
+                    kv_rows[c, kind, t] = columns(kind, c * HALF + t)
+
     queries_in.wait()
     for t in range(HALF):
         query_t[t, 0:HEAD] = to_cols(queries[:, t * block : (t + 1) * block].astype(F32)).astype(BF16)
@@ -288,12 +298,18 @@
                 lhs[s, t, at + HEAD : at + 2 * HEAD] = cols - kept
 
     flip(core)
+    for t in range(HALF):
+        weights[t, core] = dot_halves(kv_rows[core, 0, t], query_t[t])
     remote(kv_out, kv_rows.at[1 - core], pair_send.at[1], pair_recv.at[1], dp=mate).wait_recv()
     flip(1 - core)
-
+    for t in range(HALF):
+        weights[t, 1 - core] = dot_halves(kv_rows[1 - core, 0, t], query_t[t])
+
+    g_rows = HEAD // chips
+    raw_spread = []
     peaks, totals = [], []
     for t in range(HALF):
-        scores = [dot(kv_rows[s, 0, t], query_t[t]) for s in range(CORES)]
+        scores = [weights[t, s] for s in range(CORES)]
         peak = [
             functools.reduce(
                 jnp.maximum,
@@ -310,21 +326,27 @@
         total = [0.0, 0.0]
         product = 0.0
         for s in range(CORES):
-            weight = jnp.exp((scores[s] - jnp.where(in_first[s], peak[0], peak[1])) * scale)
+            weight = jnp.exp2((scores[s] - jnp.where(in_first[s], peak[0], peak[1])) * (scale * LOG2E))
             weights[t, s] = weight
             total[0] = total[0] + jnp.sum(jnp.where(in_first[s], weight, 0.0), axis=0, keepdims=True)
             total[1] = total[1] + jnp.sum(jnp.where(in_first[s], 0.0, weight), axis=0, keepdims=True)
             product = product + dot(lhs[s, t], weight.astype(BF16))
         sums[t] = product
+        for j in range(chips):
+            for q in range(2):
+                at = q * HEAD + j * g_rows
+                a_own[t, j, q] = product[at : at + g_rows].astype(BF16)
+        raw_spread.append(
+            Spread(
+                chips, chip, core,
+                lambda j, t=t: a_own.at[t, j], lambda j, t=t: a_raw.at[t, j],
+                a_raw.at[t, pl.ds(0, chips - 1)], ar_send.at[t], ar_got.at[t],
+            )
+        )
+        if t < HALF - 1:
+            raw_spread[t].start()
         peaks.append([p * scale for p in peak])
         totals.append(total)
-
-    share = split // chips
-    for j in range(chips):
-        t, at = divmod(j * share, HEAD)
-        for q in range(2):
-            a_own[j, q] = sums[t, q * HEAD + at : q * HEAD + at + share].astype(BF16)
-    raw_spread = Spread(chips, chip, core, lambda j: a_own.at[j], lambda j: a_raw.at[j], ar_send, ar_got)
     s_spread, local = [], []
     for t in range(HALF):
         u_spread[t].wait()
@@ -342,12 +364,11 @@
             Spread(
                 chips, chip, core,
                 lambda j, t=t: stats.at[t, chip], lambda j, t=t: stats.at[t, j],
-                s_send.at[t], s_got.at[t],
+                stats.at[t, pl.ds(0, chips - 1)], s_send.at[t], s_got.at[t],
             )
         )
         s_spread[t].start()
         local.append(inner_here)
-    raw_spread.start()
 
     for t in range(HALF):
         one = 0.0
@@ -359,6 +380,7 @@
             grad = weights[t, s] * (chosen - jnp.where(in_first[s], local[t][0], local[t][1]))
             one = one + dot(lhs[s, t, 2 * HEAD : 4 * HEAD], grad.astype(BF16))
         g_one[t] = one
+    raw_spread[HALF - 1].start()
 
     def whole(got, mine):
         peak = jnp.full_like(got[0][0:1], LOW)
@@ -376,7 +398,6 @@
                 inner = inner + share_of * got[d][3 * q + 2 : 3 * q + 3]
         return peak, shares, total, inner
 
-    g_rows = HEAD // chips
     g_spread = []
     for t in range(HALF):
         s_spread[t].wait()
@@ -396,27 +417,33 @@
             Spread(
                 chips, chip, core,
                 lambda j, t=t: g_own.at[t, j], lambda j, t=t: g_chip.at[t, j],
-                gr_send.at[t], gr_got.at[t],
+                g_chip.at[t, pl.ds(0, chips - 1)], gr_send.at[t], gr_got.at[t],
             )
         )
         g_spread[t].start()
 
-    raw_spread.wait()
-    a_raw[chip] = a_own[chip]
-    group = lax.div(chip, chips // HALF)
-    got = [stats[group, d] for d in range(chips)]
-    for i in range(images):
-        _, shares, total, _ = whole(got, i)
-        acc = 0.0
-        for d in range(chips):
-            for q in range(2):
-                acc = acc + shares[2 * d + q] * a_raw[d, q].astype(F32)
-        a_all[chip, i] = (acc / total).astype(BF16)
-    a_spread = Spread(chips, chip, core, lambda j: a_all.at[chip], lambda j: a_all.at[j], ag_send, ag_got)
+    for t in range(HALF):
+        raw_spread[t].wait()
+        a_raw[t, chip] = a_own[t, chip]
+        got = [stats[t, d] for d in range(chips)]
+        for i in range(images):
+            _, shares, total, _ = whole(got, i)
+            acc = 0.0
+            for d in range(chips):
+                for q in range(2):
+                    acc = acc + shares[2 * d + q] * a_raw[t, d, q].astype(F32)
+            a_all[chip, i, t] = (acc / total).astype(BF16)
+    a_spread = Spread(
+        chips, chip, core,
+        lambda j: a_all.at[chip], lambda j: a_all.at[j],
+        a_all.at[pl.ds(0, chips - 1)], ag_send.at[0], ag_got.at[0],
+    )
     a_spread.start()
 
-    def z_hop(t, k, at, target):
-        return remote(z_all.at[t, at], z_all.at[t, at], z_send.at[t, k], z_got.at[t, k], mp=target)
+    def z_hop(t, at, target):
+        return remote(z_all.at[t, at], z_all.at[t, at], z_send.at[t], z_got.at[t], mp=target)
+
+    z_next = lax.rem(z + 1, n_mp)
 
     for t in range(HALF):
         g_spread[t].wait()
@@ -425,22 +452,21 @@
             piece = piece + g_chip[t, lax.rem(chip + k, chips)].astype(F32)
         z_all[t, z] = piece.astype(BF16)
         for k in range(1, n_mp):
-            z_hop(t, k, z, lax.rem(z + k, n_mp)).start()
-
-    def g_hop(t, k, q, origin, target):
-        ref = g_all.at[t, origin[1], origin[0]]
-        at = CORES * k + q
-        return remote(ref, ref, gg_send.at[t, at], gg_got.at[t, at], dp=target[0] * CORES + target[1])
+            z_hop(t, z, lax.rem(z + k, n_mp)).start()
+
+    def g_hop(t, at, target):
+        ref = g_all.at[t, at]
+        return remote(ref, ref, gg_send.at[t], gg_got.at[t], dp=target)
 
     def other(k, q):
-        return (lax.rem(chip + k, chips), 1 - core if q else core)
+        return lax.rem(chip + k, chips) * CORES + (1 - core if q else core)
 
     hops = [(k, q) for k in list(range(1, chips)) + [0] for q in range(CORES) if k or q]
     def pick_attended():
         a_spread.wait()
-        picked = jnp.concatenate([a_all[j, 0].astype(F32) for j in range(chips)], axis=0)
+        picked = jnp.concatenate([a_all[j, 0, t].astype(F32) for t in range(HALF) for j in range(chips)], axis=0)
         for i in range(1, images):
-            option = jnp.concatenate([a_all[j, i].astype(F32) for j in range(chips)], axis=0)
+            option = jnp.concatenate([a_all[j, i, t].astype(F32) for t in range(HALF) for j in range(chips)], axis=0)
             picked = jnp.where(first == i, option, picked)
         att[core] = picked.astype(BF16)
         att_copy = remote(att.at[core], att.at[core], pair_send.at[2], pair_recv.at[2], dp=mate)
@@ -448,15 +474,13 @@
         return att_copy
 
     for t in range(HALF):
-        for k in range(1, n_mp):
-            origin = lax.rem(z + n_mp - k, n_mp)
-            z_hop(t, k, origin, origin).wait_recv()
+        z_hop(t, pl.ds(0, n_mp - 1), z_next).wait_recv()
         g_sum = z_all[t, 0].astype(F32)
         for k in range(1, n_mp):
             g_sum = g_sum + z_all[t, k].astype(F32)
-        g_all[t, core, chip] = g_sum.astype(BF16)
+        g_all[t, core * chips + chip] = g_sum.astype(BF16)
         for k, q in hops:
-            g_hop(t, k, q, (chip, core), other(k, q)).start()
+            g_hop(t, core * chips + chip, other(k, q)).start()
         if t == 0:
             att_copy = pick_attended()
 
@@ -480,22 +504,29 @@
     merged[0] = jnp.where(inside, projected.astype(F32), text[0].astype(F32)).astype(BF16)
 
     for t in range(HALF):
-        for k, q in hops:
-            origin = other(chips - k, q)
-            g_hop(t, k, q, origin, origin).wait_recv()
+        g_hop(t, pl.ds(0, n_dp - 1), mate).wait_recv()
     cols = jnp.concatenate(
-        [g_all[t, c, j].astype(F32) for c in range(CORES) for t in range(HALF) for j in range(chips)], axis=0
+        [g_all[t, c * chips + j].astype(F32) for c in range(CORES) for t in range(HALF) for j in range(chips)], axis=0
     )
     query_grad[...] = to_rows(cols, lat)
     for copy in (taken_out, kv_copy, att_copy):
         copy.wait_send()
-    for spread in u_spread + s_spread + g_spread + [raw_spread, a_spread]:
+    for spread in u_spread + s_spread + g_spread + raw_spread + [a_spread]:
         spread.drain()
     for t in range(HALF):
-        for k in range(1, n_mp):
-            z_hop(t, k, z, lax.rem(z + k, n_mp)).wait_send()
-        for k, q in hops:
-            g_hop(t, k, q, (chip, core), other(k, q)).wait_send()
+        z_hop(t, pl.ds(0, n_mp - 1), z_next).wait_send()
+        g_hop(t, pl.ds(0, n_dp - 1), mate).wait_send()
+
+
+def place(merged, query_grad, merged_out, query_grad_out, sem):
+    copies = [
+        pltpu.make_async_copy(merged, merged_out, sem.at[0]),
+        pltpu.make_async_copy(query_grad, query_grad_out, sem.at[1]),
+    ]
+    for copy in copies:
+        copy.start()
+    for copy in copies:
+        copy.wait()
 
 
 def on_device(
@@ -508,12 +539,11 @@
     chips = n_dp // CORES
     cols = PER * lat
     split = HALF * HEAD
-    share = split // chips
     g_rows = HEAD // chips
     dma = pltpu.SemaphoreType.DMA
     vmem = pl.BlockSpec(memory_space=pltpu.VMEM)
     anywhere = pl.BlockSpec(memory_space=pl.ANY)
-    return pl.pallas_call(
+    results = pl.pallas_call(
         functools.partial(kernel, (n_dp, n_mp, images, lat, tok, seq)),
         out_shape=(
             pltpu.VMEM(text_rows.shape, BF16),
@@ -543,31 +573,31 @@
             tuple(pltpu.VMEM((chips, HEAD, cols), BF16) for _ in range(HALF)),
             pltpu.VMEM((HALF, 2 * LANES, cols), BF16),
             pltpu.VMEM((HALF, chips, 8, cols), F32),
-            pltpu.VMEM((chips, 2, share, cols), BF16),
-            pltpu.VMEM((chips, 2, share, cols), BF16),
-            pltpu.VMEM((chips, images, share, cols), BF16),
+            pltpu.VMEM((HALF, chips, 2, g_rows, cols), BF16),
+            pltpu.VMEM((HALF, chips, 2, g_rows, cols), BF16),
+            pltpu.VMEM((chips, images, HALF, g_rows, cols), BF16),
             pltpu.VMEM((CORES, split, cols), BF16),
             pltpu.VMEM((HALF, chips, g_rows, cols), BF16),
             pltpu.VMEM((HALF, chips, g_rows, cols), BF16),
             pltpu.VMEM((HALF, n_mp, g_rows, cols), BF16),
-            pltpu.VMEM((HALF, CORES, chips, g_rows, cols), BF16),
+            pltpu.VMEM((HALF, CORES * chips, g_rows, cols), BF16),
             dma((11,)),
             dma((3,)),
             dma((3,)),
-            dma((HALF, chips)),
-            dma((HALF, chips)),
-            dma((HALF, chips)),
-            dma((HALF, chips)),
-            dma((chips,)),
-            dma((chips,)),
-            dma((chips,)),
-            dma((chips,)),
-            dma((HALF, chips)),
-            dma((HALF, chips)),
-            dma((HALF, n_mp)),
-            dma((HALF, n_mp)),
-            dma((HALF, n_dp)),
-            dma((HALF, n_dp)),
+            dma((HALF,)),
+            dma((HALF,)),
+            dma((HALF,)),
+            dma((HALF,)),
+            dma((HALF,)),
+            dma((HALF,)),
+            dma((1,)),
+            dma((1,)),
+            dma((HALF,)),
+            dma((HALF,)),
+            dma((HALF,)),
+            dma((HALF,)),
+            dma((HALF,)),
+            dma((HALF,)),
         ],
         compiler_params=pltpu.CompilerParams(
             collective_id=0, has_side_effects=True, vmem_limit_bytes=60 * 1024 * 1024
@@ -585,6 +615,17 @@
         text_rows,
         row_grads,
     )
+    return pl.pallas_call(
+        place,
+        out_shape=(
+            jax.ShapeDtypeStruct(text_rows.shape, BF16),
+            jax.ShapeDtypeStruct(queries.shape, F32),
+        ),
+        in_specs=[vmem, vmem],
+        out_specs=(anywhere, anywhere),
+        scratch_shapes=[dma((2,))],
+        name="place",
+    )(*[pltpu.with_memory_space_constraint(x, pltpu.VMEM) for x in results])
 
 
 def solution(mesh):

time: 32.6 us -> 30.5 us (0.936)
  local copies, waits for them, and re-layouts: 1.54 us -> 0 us
  Pallas kernels: 30.3 us -> 29.7 us
    unnamed x2 -> x0, local copies, waits for them, and re-layouts: 1.54 us -> none
    pallas_call x1, Pallas kernels: 30.3 us -> 28.7 us  [on_device(): pl.pallas_call(functools.partial(kernel, (n_dp, n_mp, images, lat, tok, s...]
    pallas_call x0 -> x1, Pallas kernels: none -> 0.94 us  [on_device(): pl.pallas_call(place, out_shape=(jax.ShapeDtypeStruct(text_rows.shape, BF...]
where the time goes in v2:
time: 30.5 us; the launch traced here: 30.3 us
  Pallas kernels  29.7 us (97%)
  between operations  0.64 us (2%)
    pallas_call x1, Pallas kernels, on_device(): pl.pallas_call(functools.partial(kernel, (n_dp, n_mp, images, lat, tok, s...  28.7 us
    pallas_call x1, Pallas kernels, on_device(): pl.pallas_call(place, out_shape=(jax.ShapeDtypeStruct(text_rows.shape, BF...  0.94 us

profile of v2, /device:TPU:0, one launch (start us, length us, event | category | flops | bytes accessed | tf_op | source)
XLA Modules:
  0.0 30.3 jit_solution(4225404974056103974)
XLA Ops:
  0.6 28.7 %resampler.1 = (bf16[1,128,2048]{2,1,0:T(8,128)(2,1)S(1)}, f32[64,1536]{1,0:T(8,128)S(1)}) custom-call(s32[1,2]{1,0:T(1,128)} %tiles_hbm.1, s32[1,2]{1,0:T(1,128)} %slots_hbm.1, f32[1152]{0:T(1024)} %gain_hbm.1, bf16[64,1536]{1,0:T(8,128)(2,1)} %queries_hbm.1, bf16[1,512,1152]{2,1,0:T(8,128)(2,1)} %features_hbm.1, bf16[1152,384]{1,0:T(8,128)(2,1)} %wk_hbm.1, ...), custom_call_target="tpu_custom_call" | custom-call | tf_op jit(solution)/shard_map/resampler/pallas_call | solution.py:546
  29.4 0.9 %place.1 = (bf16[1,128,2048]{2,1,0:T(8,128)(2,1)}, f32[64,1536]{1,0:T(8,128)}) custom-call(bf16[1,128,2048]{2,1,0:T(8,128)(2,1)S(1)} %get-tuple-element.4.merged, f32[64,1536]{1,0:T(8,128)S(1)} %get-tuple-element.5.query_grad), custom_call_target="tpu_custom_call" | custom-call | tf_op jit(solution)/shard_map/place/pallas_call | solution.py:618

commit v3 on v2

--- a/solution.py
+++ b/solution.py
@@ -240,21 +240,28 @@
     remote(taken.at[1 - core], taken.at[1 - core], pair_send.at[0], pair_recv.at[0], dp=mate).wait_recv()
     wo_near.wait()
     flipped = (taken[0] + taken[1]).T
-    u_spread = []
+    most_rows = 6 * tok
+
+    def u_goes(source, target):
+        reach = jnp.where(target == 0, (most_rows - 1) // chip_rows, (chip_rows + most_rows - 2) // chip_rows)
+        return (target < source) & (source - target <= reach)
+
+    def u_hop(t, source, target):
+        ref = u_all[t].at[source]
+        return remote(ref, ref, u_send.at[t, target], u_got.at[t, source], dp=target * CORES + core)
+
     for t in range(HALF):
         at = pl.multiple_of((core * HALF + t) * block, block)
         up = dot_halves(wo[pl.ds(at, block), :], flipped)
         u_all[t][chip] = jnp.concatenate(
             [up[c * HEAD : (c + 1) * HEAD] for c in range(PER)], axis=1
         ).astype(BF16)
-        u_spread.append(
-            Spread(
-                chips, chip, core,
-                lambda j, t=t: u_all[t].at[chip], lambda j, t=t: u_all[t].at[j],
-                u_all[t].at[pl.ds(0, chips - 1)], u_send.at[t], u_got.at[t],
-            )
-        )
-        u_spread[t].start()
+        for target in range(chips):
+
+            @pl.when(u_goes(chip, target))
+            def _():
+                u_hop(t, chip, target).start()
+
     wv_in.wait()
     both[:, early:] = dot_halves(features[0], wkv[:, early:]).astype(BF16)
     pad = jnp.zeros((tok, LANES - HEAD), BF16)
@@ -263,16 +270,20 @@
         at = kind * KVH * HEAD + g * HEAD
         return jnp.concatenate([both[:, at : at + HEAD], pad], axis=1)
 
-    for c in range(CORES):
-
-        @pl.when(core == c)
-        def _():
-            for kind in range(2):
+    def kv_hop(kind, at):
+        return remote(
+            kv_out.at[kind], kv_rows.at[at, kind], pair_send.at[2 + kind], pair_recv.at[2 + kind], dp=mate
+        )
+
+    for kind in range(2):
+        for c in range(CORES):
+
+            @pl.when(core == c)
+            def _():
                 for t in range(HALF):
                     kv_out[kind, t] = columns(kind, (1 - c) * HALF + t)
 
-    kv_copy = remote(kv_out, kv_rows.at[core], pair_send.at[1], pair_recv.at[1], dp=mate)
-    kv_copy.start()
+        kv_hop(kind, core).start()
     for c in range(CORES):
 
         @pl.when(core == c)
@@ -300,10 +311,11 @@
     flip(core)
     for t in range(HALF):
         weights[t, core] = dot_halves(kv_rows[core, 0, t], query_t[t])
-    remote(kv_out, kv_rows.at[1 - core], pair_send.at[1], pair_recv.at[1], dp=mate).wait_recv()
+    kv_hop(0, 1 - core).wait_recv()
+    for t in range(HALF):
+        weights[t, 1 - core] = dot_halves(kv_rows[1 - core, 0, t], query_t[t])
+    kv_hop(1, 1 - core).wait_recv()
     flip(1 - core)
-    for t in range(HALF):
-        weights[t, 1 - core] = dot_halves(kv_rows[1 - core, 0, t], query_t[t])
 
     g_rows = HEAD // chips
     raw_spread = []
@@ -349,7 +361,12 @@
         totals.append(total)
     s_spread, local = [], []
     for t in range(HALF):
-        u_spread[t].wait()
+        for source in range(chips):
+
+            @pl.when(u_goes(source, chip))
+            def _():
+                u_hop(t, source, chip).wait_recv()
+
         u_pair[t, HEAD:LANES] = jnp.zeros((LANES - HEAD, u_pair.shape[2]), BF16)
         u_pair[t, LANES + HEAD : 2 * LANES] = jnp.zeros((LANES - HEAD, u_pair.shape[2]), BF16)
         rows_here, inner_here = [], []
@@ -469,7 +486,7 @@
             option = jnp.concatenate([a_all[j, i, t].astype(F32) for t in range(HALF) for j in range(chips)], axis=0)
             picked = jnp.where(first == i, option, picked)
         att[core] = picked.astype(BF16)
-        att_copy = remote(att.at[core], att.at[core], pair_send.at[2], pair_recv.at[2], dp=mate)
+        att_copy = remote(att.at[core], att.at[core], pair_send.at[1], pair_recv.at[1], dp=mate)
         att_copy.start()
         return att_copy
 
@@ -497,7 +514,7 @@
         return dot(placed, wo[half_rows(c), :])
 
     near = project(core)
-    remote(att.at[1 - core], att.at[1 - core], pair_send.at[2], pair_recv.at[2], dp=mate).wait_recv()
+    remote(att.at[1 - core], att.at[1 - core], pair_send.at[1], pair_recv.at[1], dp=mate).wait_recv()
     projected = (near + project(1 - core)).astype(BF16)
     row_at = lax.broadcasted_iota(jnp.int32, (seq, 1), 0)
     inside = (row_at >= slot) & (row_at < slot + lat)
@@ -509,9 +526,16 @@
         [g_all[t, c * chips + j].astype(F32) for c in range(CORES) for t in range(HALF) for j in range(chips)], axis=0
     )
     query_grad[...] = to_rows(cols, lat)
-    for copy in (taken_out, kv_copy, att_copy):
+    for copy in (taken_out, kv_hop(0, core), kv_hop(1, core), att_copy):
         copy.wait_send()
-    for spread in u_spread + s_spread + g_spread + raw_spread + [a_spread]:
+    for t in range(HALF):
+        for target in range(chips):
+
+            @pl.when(u_goes(chip, target))
+            def _():
+                u_hop(t, chip, target).wait_send()
+
+    for spread in s_spread + g_spread + raw_spread + [a_spread]:
         spread.drain()
     for t in range(HALF):
         z_hop(t, pl.ds(0, n_mp - 1), z_next).wait_send()
@@ -582,10 +606,10 @@
             pltpu.VMEM((HALF, n_mp, g_rows, cols), BF16),
             pltpu.VMEM((HALF, CORES * chips, g_rows, cols), BF16),
             dma((11,)),
-            dma((3,)),
-            dma((3,)),
-            dma((HALF,)),
-            dma((HALF,)),
+            dma((4,)),
+            dma((4,)),
+            dma((HALF, chips)),
+            dma((HALF, chips)),
             dma((HALF,)),
             dma((HALF,)),
             dma((HALF,)),

time: 30.5 us -> 29.6 us (0.970)
  Pallas kernels: 29.7 us -> 28.8 us
    pallas_call x1, Pallas kernels: 28.7 us -> 27.9 us  [on_device(): pl.pallas_call(functools.partial(kernel, (n_dp, n_mp, images, lat, tok, s...]
where the time goes in v3:
time: 29.6 us; the launch traced here: 29.5 us
  Pallas kernels  28.8 us (97%)
  between operations  0.64 us (2%)
    pallas_call x1, Pallas kernels, on_device(): pl.pallas_call(functools.partial(kernel, (n_dp, n_mp, images, lat, tok, s...  27.9 us
    pallas_call x1, Pallas kernels, on_device(): pl.pallas_call(place, out_shape=(jax.ShapeDtypeStruct(text_rows.shape, BF...  0.94 us

profile of v3, /device:TPU:0, one launch (start us, length us, event | category | flops | bytes accessed | tf_op | source)
XLA Modules:
  0.0 29.5 jit_solution(6213505736262984561)
XLA Ops:
  0.6 27.9 %resampler.1 = (bf16[1,128,2048]{2,1,0:T(8,128)(2,1)S(1)}, f32[64,1536]{1,0:T(8,128)S(1)}) custom-call(s32[1,2]{1,0:T(1,128)} %tiles_hbm.1, s32[1,2]{1,0:T(1,128)} %slots_hbm.1, f32[1152]{0:T(1024)} %gain_hbm.1, bf16[64,1536]{1,0:T(8,128)(2,1)} %queries_hbm.1, bf16[1,512,1152]{2,1,0:T(8,128)(2,1)} %features_hbm.1, bf16[1152,384]{1,0:T(8,128)(2,1)} %wk_hbm.1, ...), custom_call_target="tpu_custom_call" | custom-call | tf_op jit(solution)/shard_map/resampler/pallas_call | solution.py:570
  28.5 0.9 %place.1 = (bf16[1,128,2048]{2,1,0:T(8,128)(2,1)}, f32[64,1536]{1,0:T(8,128)}) custom-call(bf16[1,128,2048]{2,1,0:T(8,128)(2,1)S(1)} %get-tuple-element.4.merged, f32[64,1536]{1,0:T(8,128)S(1)} %get-tuple-element.5.query_grad), custom_call_target="tpu_custom_call" | custom-call | tf_op jit(solution)/shard_map/place/pallas_call | solution.py:642
